TPU v7x, 128 devices: a whole 4x4x4 slice. The times are simulated.
128 devices in a mesh: prompt: 8 (over y_hi, z), slot: 16 (over x, y_lo, core).
Axes of the slice: x: 4, y: 4 (y_hi: 2, y_lo: 2; y = y_hi * 2 + y_lo), z: 4, core: 2. Of those that a mesh axis runs over, the one named last changes fastest.
Arguments:
- patch_kv: bfloat16 [8, 256, 128, 2048], P('prompt', 'slot'), may hold values from -6 to 6
- routes: int32 [8, 256], P('prompt', 'slot'), may hold values from -1 to 15, as said below
- prefix_kv: bfloat16 [8, 512, 2048], P('prompt', None, 'slot'), may hold values from -4 to 4
- prefix_len: int32 [8], P('prompt'), may hold values from 1 to 512, 3072 in all
- queries: bfloat16 [8, 16, 256, 8192], P('prompt', 'slot'), may hold values from -160 to 160
- suffix_kv: bfloat16 [8, 16, 256, 2048], P('prompt', 'slot'), may hold values from -6 to 6
- score_head: float32 [8192], replicated, may hold values from -0.0625 to 0.0625
Outputs:
- context: bfloat16 [8, 16, 256, 8192], P('prompt', 'slot')
- advantage: float32 [8, 16], P('prompt', 'slot')
Inputs may be any that keep to these rules, and one draw needn't show every extreme that they name: `routes`: in the list of one generating device each judge index appears at most once, and in one prompt's lists each judge index appears exactly 8 times; -1 marks an empty slot.
All inputs are finite; a program needn't handle non-finite values. No bound on the sum of `prefix_len` on one device may be relied on, other than what follows from the above.
Results may differ from a plain program's by a relative error of at most 0.005.
Values may be sent and summed in bfloat16 or wider, within the bound.
A program may use at most 128 MiB of HBM per device.

v0:
```python
import math

import jax
import jax.numpy as jnp
from jax import lax
from jax.sharding import PartitionSpec as P

HEADS = 64
KVH = 8
HD = 128


def per_device(patch_kv, routes, prefix_kv, prefix_len, queries, suffix_kv, score_head):
    slot_count = lax.axis_size("slot")
    prompt_count = lax.axis_size("prompt")
    tile_rows = patch_kv.shape[2]
    width_kv = patch_kv.shape[3]
    suffix_rows = queries.shape[2]
    prefix_rows = prefix_kv.shape[1]
    groups = HEADS // KVH
    factor = 1.0 / math.sqrt(HD)
    judges = jnp.arange(slot_count, dtype=jnp.int32)
    matches = routes[0][None, :] == judges[:, None]
    outgoing = jnp.einsum(
        "dk,krc->drc", matches.astype(jnp.bfloat16), patch_kv[0], preferred_element_type=jnp.float32
    ).astype(jnp.bfloat16)
    carried = jnp.any(matches, axis=1).astype(jnp.bfloat16)
    incoming, arrived = (
        lax.all_to_all(outgoing, "slot", split_axis=0, concat_axis=0, tiled=True),
        lax.all_to_all(carried, "slot", split_axis=0, concat_axis=0, tiled=True),
    )
    live = arrived > 0
    tiles_kept = slot_count // 2
    kept_index = jnp.nonzero(live, size=tiles_kept)[0].astype(jnp.int32)
    image_rows = incoming[kept_index].reshape(tiles_kept * tile_rows, width_kv)
    prefix_whole = lax.all_gather(prefix_kv[0], "slot", axis=1, tiled=True)
    rows_all = jnp.concatenate([prefix_whole, image_rows, suffix_kv[0, 0]], axis=0)
    image_count = image_rows.shape[0]
    columns = jnp.arange(prefix_rows + image_count + suffix_rows, dtype=jnp.int32)[None, :]
    positions = jnp.arange(suffix_rows, dtype=jnp.int32)[:, None]
    allowed = jnp.where(
        columns < prefix_rows,
        columns < prefix_len[0],
        jnp.where(
            columns < prefix_rows + image_count,
            True,
            columns - prefix_rows - image_count <= positions,
        ),
    )
    grouped_queries = jnp.transpose(
        queries[0, 0].reshape(suffix_rows, KVH, groups, HD), (1, 2, 0, 3)
    )

    def one_group(group):
        query_rows = lax.dynamic_index_in_dim(grouped_queries, group, 0, keepdims=False)
        key_rows = lax.dynamic_slice_in_dim(rows_all, group * HD, HD, 1)
        value_rows = lax.dynamic_slice_in_dim(rows_all, (KVH + group) * HD, HD, 1)
        scores = (
            jnp.einsum("gsd,kd->gsk", query_rows, key_rows, preferred_element_type=jnp.float32)
            * factor
        )
        scores = jnp.where(allowed[None, :, :], scores, -1e30)
        peak = jnp.max(scores, axis=-1, keepdims=True)
        weights = jnp.exp(scores - peak)
        totals = jnp.sum(weights, axis=-1, keepdims=True)
        rounded = weights.astype(jnp.bfloat16)
        mixed = jnp.einsum("gsk,kd->gsd", rounded, value_rows, preferred_element_type=jnp.float32)
        return mixed / totals

    blocks = lax.map(one_group, jnp.arange(KVH, dtype=jnp.int32))
    context = (
        jnp.transpose(blocks, (2, 0, 1, 3)).reshape(suffix_rows, HEADS * HD).astype(jnp.bfloat16)
    )
    score = jnp.dot(
        context[suffix_rows - 1].astype(jnp.float32),
        score_head,
        precision=lax.Precision.HIGHEST,
        preferred_element_type=jnp.float32,
    )
    centre = lax.psum(score, "slot") / slot_count
    deviation = score - centre
    spread = lax.psum(deviation * deviation, ("prompt", "slot")) / (prompt_count * slot_count)
    advantage = deviation / jnp.sqrt(spread + 1e-06)
    return (context[None, None], advantage.reshape(1, 1))


def solution(mesh):
    placed = (
        P("prompt", "slot", None, None),
        P("prompt", "slot"),
        P("prompt", None, "slot"),
        P("prompt"),
        P("prompt", "slot", None, None),
        P("prompt", "slot", None, None),
        P(),
    )
    return jax.shard_map(
        per_device,
        mesh=mesh,
        in_specs=placed,
        out_specs=(P("prompt", "slot", None, None), P("prompt", "slot")),
        check_vma=False,
    )
```

profile of v0, /device:TPU:1, one launch (start us, length us, event | category | flops | bytes accessed | tf_op | source)
XLA Modules:
  0.0 516.3 jit_solution(6852370807934875014)
XLA Ops:
  8.6 6.8 %all-to-all-start.1 = ((bf16[16,1,1]{2,1,0:T(2,128)(2,1)}), bf16[16,1,1]{2,1,0:T(2,128)(2,1)S(1)}, u32[]{:S(2)}, u32[]{:S(2)}) async-start(bf16[16,1,1]{2,1,0:T(2,128)(2,1)} %copy.28), calls=%async_computation.1 | async-start | bytes 16384 | tf_op jit(solution)/shard_map/all_to_all | solution.py:30
  15.5 16.1 %fusion.25 = bf16[16,128,2048]{2,0,1:T(8,128)(2,1)} fusion(bf16[16,128,2048]{2,1,0:T(8,128)(2,1)} %bitcast.58, s32[16]{0:T(128)} %bitcast.63), kind=kOutput, calls=%fused_computation.29 | convolution fusion | flops 138412288 | bytes 16777280 | tf_op jit(solution)/shard_map/dk,krc->drc/dot_general | solution.py:24
  31.6 11.4 %copy.27 = bf16[16,128,2048]{2,1,0:T(8,128)(2,1)} copy(bf16[16,128,2048]{2,0,1:T(8,128)(2,1)} %fusion.25) | data formatting | bytes 16777216 | tf_op jit(solution)/shard_map/convert_element_type | solution.py:26
  43.0 5.7 %all-to-all-start = ((bf16[16,128,2048]{2,1,0:T(8,128)(2,1)}), bf16[16,128,2048]{2,1,0:T(8,128)(2,1)}, u32[]{:S(2)}, u32[]{:S(2)}) async-start(bf16[16,128,2048]{2,1,0:T(8,128)(2,1)} %copy.27), calls=%async_computation | async-start | bytes 16777216 | tf_op jit(solution)/shard_map/all_to_all | solution.py:29
  50.1 6.5 %copy.25 = bf16[1,1,256,8192]{2,3,1,0:T(8,128)(2,1)} copy(bf16[1,1,256,8192]{3,2,1,0:T(8,128)(2,1)} %param.13) | data formatting | bytes 8388608 | tf_op args[4]
  58.9 122.2 %all-to-all-done = bf16[16,128,2048]{2,1,0:T(8,128)(2,1)} async-done(((bf16[16,128,2048]{2,1,0:T(8,128)(2,1)}), bf16[16,128,2048]{2,1,0:T(8,128)(2,1)}, u32[]{:S(2)}, u32[]{:S(2)}) %all-to-all-start) | async-done | bytes 8388640 | tf_op jit(solution)/shard_map/all_to_all | solution.py:29
  181.0 6.2 %gather_fusion = bf16[8,128,2048]{2,1,0:T(8,128)(2,1)} fusion(bf16[16,128,2048]{2,1,0:T(8,128)(2,1)} %all-to-all-done, s32[1024]{0:T(1024)S(1)} %pad_clamp_fusion), kind=kCustom, calls=%fused_computation | custom fusion | bytes 8388640 | tf_op jit(solution)/shard_map/gather | solution.py:35
  187.2 6.2 %pad_maximum_fusion = bf16[1792,2048]{1,0:T(8,128)(2,1)} fusion(bf16[256,2048]{1,0:T(8,128)(2,1)S(1)} %bitcast.60, bf16[1024,2048]{1,0:T(8,128)(2,1)} %bitcast.56, bf16[512,2048]{1,0:T(8,128)(2,1)} %bitcast.59), kind=kLoop, calls=%fused_computation.28 | loop fusion | flops 22020096 | bytes 14680064 | tf_op jit(solution)/shard_map/concatenate | solution.py:37
  193.4 205.8 %while.11 = (s32[]{:T(128)}, bf16[8,8,256,128]{3,1,0,2:T(8,128)(2,1)}, s32[8]{0:T(128)S(1)}, bf16[8,8,256,128]{2,3,1,0:T(8,128)(2,1)}, bf16[1792,2048]{1,0:T(8,1...) while((s32[]{:T(128)}, ...), condition=%wide.region_8.9_spmd.clone, body=%wide.region_5.8_spmd.clone.sunk | while | flops 1921314816 | bytes 107664440 | solution.py:70
  197.2 4.3 fusion.47
  201.6 5.2 %copy-done = f32[8,256,1792]{2,1,0:T(8,128)} copy-done((f32[8,256,1792]{2,1,0:T(8,128)}, f32[8,256,1792]{2,1,0:T(8,128)S(1)}, u32[]{:S(2)}) %copy-start) | copy-done | bytes 14680088 | tf_op jit(solution)/shard_map/while
  206.8 4.0 fusion.48
  210.8 7.2 %divide_bitcast_fusion.2 = bf16[1,8,256,128]{3,2,1,0:T(8,128)(2,1)S(1)} fusion(f32[8,256,1792]{2,1,0:T(8,128)} %copy-done, f32[8,256]{1,0:T(8,128)S(1)} %get-tuple-element.166, pred[256,1792]{1,0:T(8,128)(4,1)S(1)} %fusion.46, f32[8,256]{1,0:T(8,128)S(1)} %fusion.48, bf16[1792,2048]{1,0:T(8,128)(2,1)} %get-tuple-element.199, s32[]{:T(128)S(6)} %select_n.139), kind=kOutput, calls=%fused_computation.14.clone.1 | convolution fusion | flops 954728448 | bytes 16138244 | tf_op jit(solution)/shard_map/while/body/eval_jaxpr/gsk,kd->gsd/dot_general | solution.py:67
  217.9 1.2 copy_dynamic-update-slice_fusion.2
  223.0 4.3 fusion.47
  227.3 5.2 %copy-done = f32[8,256,1792]{2,1,0:T(8,128)} copy-done((f32[8,256,1792]{2,1,0:T(8,128)}, f32[8,256,1792]{2,1,0:T(8,128)S(1)}, u32[]{:S(2)}) %copy-start) | copy-done | bytes 14680088 | tf_op jit(solution)/shard_map/while
  232.5 4.0 fusion.48
  236.5 7.2 %divide_bitcast_fusion.2 = bf16[1,8,256,128]{3,2,1,0:T(8,128)(2,1)S(1)} fusion(f32[8,256,1792]{2,1,0:T(8,128)} %copy-done, f32[8,256]{1,0:T(8,128)S(1)} %get-tuple-element.166, pred[256,1792]{1,0:T(8,128)(4,1)S(1)} %fusion.46, f32[8,256]{1,0:T(8,128)S(1)} %fusion.48, bf16[1792,2048]{1,0:T(8,128)(2,1)} %get-tuple-element.199, s32[]{:T(128)S(6)} %select_n.139), kind=kOutput, calls=%fused_computation.14.clone.1 | convolution fusion | flops 954728448 | bytes 16138244 | tf_op jit(solution)/shard_map/while/body/eval_jaxpr/gsk,kd->gsd/dot_general | solution.py:67
  248.7 4.4 fusion.47
  253.0 5.2 %copy-done = f32[8,256,1792]{2,1,0:T(8,128)} copy-done((f32[8,256,1792]{2,1,0:T(8,128)}, f32[8,256,1792]{2,1,0:T(8,128)S(1)}, u32[]{:S(2)}) %copy-start) | copy-done | bytes 14680088 | tf_op jit(solution)/shard_map/while
  258.2 4.0 fusion.48
  262.2 7.2 %divide_bitcast_fusion.2 = bf16[1,8,256,128]{3,2,1,0:T(8,128)(2,1)S(1)} fusion(f32[8,256,1792]{2,1,0:T(8,128)} %copy-done, f32[8,256]{1,0:T(8,128)S(1)} %get-tuple-element.166, pred[256,1792]{1,0:T(8,128)(4,1)S(1)} %fusion.46, f32[8,256]{1,0:T(8,128)S(1)} %fusion.48, bf16[1792,2048]{1,0:T(8,128)(2,1)} %get-tuple-element.199, s32[]{:T(128)S(6)} %select_n.139), kind=kOutput, calls=%fused_computation.14.clone.1 | convolution fusion | flops 954728448 | bytes 16138244 | tf_op jit(solution)/shard_map/while/body/eval_jaxpr/gsk,kd->gsd/dot_general | solution.py:67
  274.4 4.3 fusion.47
  278.8 5.2 %copy-done = f32[8,256,1792]{2,1,0:T(8,128)} copy-done((f32[8,256,1792]{2,1,0:T(8,128)}, f32[8,256,1792]{2,1,0:T(8,128)S(1)}, u32[]{:S(2)}) %copy-start) | copy-done | bytes 14680088 | tf_op jit(solution)/shard_map/while
  284.0 4.0 fusion.48
  288.0 7.2 %divide_bitcast_fusion.2 = bf16[1,8,256,128]{3,2,1,0:T(8,128)(2,1)S(1)} fusion(f32[8,256,1792]{2,1,0:T(8,128)} %copy-done, f32[8,256]{1,0:T(8,128)S(1)} %get-tuple-element.166, pred[256,1792]{1,0:T(8,128)(4,1)S(1)} %fusion.46, f32[8,256]{1,0:T(8,128)S(1)} %fusion.48, bf16[1792,2048]{1,0:T(8,128)(2,1)} %get-tuple-element.199, s32[]{:T(128)S(6)} %select_n.139), kind=kOutput, calls=%fused_computation.14.clone.1 | convolution fusion | flops 954728448 | bytes 16138244 | tf_op jit(solution)/shard_map/while/body/eval_jaxpr/gsk,kd->gsd/dot_general | solution.py:67
  300.2 4.3 fusion.47
  304.5 5.2 %copy-done = f32[8,256,1792]{2,1,0:T(8,128)} copy-done((f32[8,256,1792]{2,1,0:T(8,128)}, f32[8,256,1792]{2,1,0:T(8,128)S(1)}, u32[]{:S(2)}) %copy-start) | copy-done | bytes 14680088 | tf_op jit(solution)/shard_map/while
  309.7 4.0 fusion.48
  313.7 7.2 %divide_bitcast_fusion.2 = bf16[1,8,256,128]{3,2,1,0:T(8,128)(2,1)S(1)} fusion(f32[8,256,1792]{2,1,0:T(8,128)} %copy-done, f32[8,256]{1,0:T(8,128)S(1)} %get-tuple-element.166, pred[256,1792]{1,0:T(8,128)(4,1)S(1)} %fusion.46, f32[8,256]{1,0:T(8,128)S(1)} %fusion.48, bf16[1792,2048]{1,0:T(8,128)(2,1)} %get-tuple-element.199, s32[]{:T(128)S(6)} %select_n.139), kind=kOutput, calls=%fused_computation.14.clone.1 | convolution fusion | flops 954728448 | bytes 16138244 | tf_op jit(solution)/shard_map/while/body/eval_jaxpr/gsk,kd->gsd/dot_general | solution.py:67
  325.9 4.3 fusion.47
  330.2 5.2 %copy-done = f32[8,256,1792]{2,1,0:T(8,128)} copy-done((f32[8,256,1792]{2,1,0:T(8,128)}, f32[8,256,1792]{2,1,0:T(8,128)S(1)}, u32[]{:S(2)}) %copy-start) | copy-done | bytes 14680088 | tf_op jit(solution)/shard_map/while
  335.4 4.0 fusion.48
  339.4 7.2 %divide_bitcast_fusion.2 = bf16[1,8,256,128]{3,2,1,0:T(8,128)(2,1)S(1)} fusion(f32[8,256,1792]{2,1,0:T(8,128)} %copy-done, f32[8,256]{1,0:T(8,128)S(1)} %get-tuple-element.166, pred[256,1792]{1,0:T(8,128)(4,1)S(1)} %fusion.46, f32[8,256]{1,0:T(8,128)S(1)} %fusion.48, bf16[1792,2048]{1,0:T(8,128)(2,1)} %get-tuple-element.199, s32[]{:T(128)S(6)} %select_n.139), kind=kOutput, calls=%fused_computation.14.clone.1 | convolution fusion | flops 954728448 | bytes 16138244 | tf_op jit(solution)/shard_map/while/body/eval_jaxpr/gsk,kd->gsd/dot_general | solution.py:67
  346.6 1.2 copy_dynamic-update-slice_fusion.2
  351.6 4.3 fusion.47
  355.9 5.2 %copy-done = f32[8,256,1792]{2,1,0:T(8,128)} copy-done((f32[8,256,1792]{2,1,0:T(8,128)}, f32[8,256,1792]{2,1,0:T(8,128)S(1)}, u32[]{:S(2)}) %copy-start) | copy-done | bytes 14680088 | tf_op jit(solution)/shard_map/while
  361.1 4.0 fusion.48
  365.1 7.2 %divide_bitcast_fusion.2 = bf16[1,8,256,128]{3,2,1,0:T(8,128)(2,1)S(1)} fusion(f32[8,256,1792]{2,1,0:T(8,128)} %copy-done, f32[8,256]{1,0:T(8,128)S(1)} %get-tuple-element.166, pred[256,1792]{1,0:T(8,128)(4,1)S(1)} %fusion.46, f32[8,256]{1,0:T(8,128)S(1)} %fusion.48, bf16[1792,2048]{1,0:T(8,128)(2,1)} %get-tuple-element.199, s32[]{:T(128)S(6)} %select_n.139), kind=kOutput, calls=%fused_computation.14.clone.1 | convolution fusion | flops 954728448 | bytes 16138244 | tf_op jit(solution)/shard_map/while/body/eval_jaxpr/gsk,kd->gsd/dot_general | solution.py:67
  377.3 4.3 fusion.47
  381.6 5.2 %copy-done = f32[8,256,1792]{2,1,0:T(8,128)} copy-done((f32[8,256,1792]{2,1,0:T(8,128)}, f32[8,256,1792]{2,1,0:T(8,128)S(1)}, u32[]{:S(2)}) %copy-start) | copy-done | bytes 14680088 | tf_op jit(solution)/shard_map/while
  386.8 4.0 fusion.48
  390.8 7.2 %divide_bitcast_fusion.2 = bf16[1,8,256,128]{3,2,1,0:T(8,128)(2,1)S(1)} fusion(f32[8,256,1792]{2,1,0:T(8,128)} %copy-done, f32[8,256]{1,0:T(8,128)S(1)} %get-tuple-element.166, pred[256,1792]{1,0:T(8,128)(4,1)S(1)} %fusion.46, f32[8,256]{1,0:T(8,128)S(1)} %fusion.48, bf16[1792,2048]{1,0:T(8,128)(2,1)} %get-tuple-element.199, s32[]{:T(128)S(6)} %select_n.139), kind=kOutput, calls=%fused_computation.14.clone.1 | convolution fusion | flops 954728448 | bytes 16138244 | tf_op jit(solution)/shard_map/while/body/eval_jaxpr/gsk,kd->gsd/dot_general | solution.py:67
  398.0 1.2 copy_dynamic-update-slice_fusion.2
  399.2 1.3 fusion.28
  400.6 27.7 %psum.14 = f32[]{:T(128)} all-reduce(f32[]{:T(128)} %fusion.28), channel_id=1, replica_groups=mesh['prompt'=8,'slot'=16] {'slot'}, use_global_device_ids=true, to_apply=%region_9.10 | all-reduce | flops 1 | bytes 8 | tf_op jit(solution)/shard_map/psum | solution.py:80
  429.6 7.3 %convert_element_type.65 = bf16[1,1,256,8192]{3,2,1,0:T(8,128)(2,1)} reshape(bf16[256,8,8,128]{3,2,1,0:T(8,128)(2,1)} %bitcast.40) | data formatting | bytes 8388608 | tf_op jit(solution)/shard_map/convert_element_type | solution.py:72
  436.8 70.7 %psum.15 = f32[]{:T(128)} all-reduce(f32[]{:T(128)S(6)} %mul.12), channel_id=1, replica_groups=mesh['prompt'=8,'slot'=16] {'prompt','slot'}, use_global_device_ids=true, to_apply=%region_10.11 | all-reduce | flops 1 | bytes 8 | tf_op jit(solution)/shard_map/psum | solution.py:82
  (54 shorter events, 18.8 us)
Async XLA Ops:
  8.6 34.4 %all-to-all-start.1 = ((bf16[16,1,1]{2,1,0:T(2,128)(2,1)}), bf16[16,1,1]{2,1,0:T(2,128)(2,1)S(1)}, u32[]{:S(2)}, u32[]{:S(2)}) async-start(bf16[16,1,1]{2,1,0:T(2,128)(2,1)} %copy.28), calls=%async_computation.1 | async-start | bytes 16384 | tf_op jit(solution)/shard_map/all_to_all | solution.py:30
  43.0 138.0 %all-to-all-start = ((bf16[16,128,2048]{2,1,0:T(8,128)(2,1)}), bf16[16,128,2048]{2,1,0:T(8,128)(2,1)}, u32[]{:S(2)}, u32[]{:S(2)}) async-start(bf16[16,128,2048]{2,1,0:T(8,128)(2,1)} %copy.27), calls=%async_computation | async-start | bytes 16777216 | tf_op jit(solution)/shard_map/all_to_all | solution.py:29
  48.7 138.5 %all-gather.3.cloned.1.call-start = ((), (), s32[]{:S(2)}) async-start(), calls=%async_computation.2 | async-start | bytes 2228224 | tf_op jit(solution)/shard_map/all_gather | solution.py:36
  50.1 137.1 %copy-start.1 = (bf16[1,1,256,2048]{3,2,1,0:T(8,128)(2,1)S(1)}, bf16[1,1,256,2048]{3,2,1,0:T(8,128)(2,1)}, u32[]{:S(2)}) copy-start(bf16[1,1,256,2048]{3,2,1,0:T(8,128)(2,1)} %param.14) | copy-start | bytes 3145732
  193.4 205.8 %copy-start.2 = (f32[8192]{0:T(1024)S(1)}, f32[8192]{0:T(1024)}, u32[]{:S(2)}) copy-start(f32[8192]{0:T(1024)} %param.15) | copy-start | bytes 98308
  201.5 5.2 %copy-start = (f32[8,256,1792]{2,1,0:T(8,128)}, f32[8,256,1792]{2,1,0:T(8,128)S(1)}, u32[]{:S(2)}) copy-start(f32[8,256,1792]{2,1,0:T(8,128)S(1)} %get-tuple-element.165) | copy-start | bytes 44040196 | tf_op jit(solution)/shard_map/while
  227.3 5.2 %copy-start = (f32[8,256,1792]{2,1,0:T(8,128)}, f32[8,256,1792]{2,1,0:T(8,128)S(1)}, u32[]{:S(2)}) copy-start(f32[8,256,1792]{2,1,0:T(8,128)S(1)} %get-tuple-element.165) | copy-start | bytes 44040196 | tf_op jit(solution)/shard_map/while
  253.0 5.2 %copy-start = (f32[8,256,1792]{2,1,0:T(8,128)}, f32[8,256,1792]{2,1,0:T(8,128)S(1)}, u32[]{:S(2)}) copy-start(f32[8,256,1792]{2,1,0:T(8,128)S(1)} %get-tuple-element.165) | copy-start | bytes 44040196 | tf_op jit(solution)/shard_map/while
  278.8 5.2 %copy-start = (f32[8,256,1792]{2,1,0:T(8,128)}, f32[8,256,1792]{2,1,0:T(8,128)S(1)}, u32[]{:S(2)}) copy-start(f32[8,256,1792]{2,1,0:T(8,128)S(1)} %get-tuple-element.165) | copy-start | bytes 44040196 | tf_op jit(solution)/shard_map/while
  304.5 5.2 %copy-start = (f32[8,256,1792]{2,1,0:T(8,128)}, f32[8,256,1792]{2,1,0:T(8,128)S(1)}, u32[]{:S(2)}) copy-start(f32[8,256,1792]{2,1,0:T(8,128)S(1)} %get-tuple-element.165) | copy-start | bytes 44040196 | tf_op jit(solution)/shard_map/while
  330.2 5.2 %copy-start = (f32[8,256,1792]{2,1,0:T(8,128)}, f32[8,256,1792]{2,1,0:T(8,128)S(1)}, u32[]{:S(2)}) copy-start(f32[8,256,1792]{2,1,0:T(8,128)S(1)} %get-tuple-element.165) | copy-start | bytes 44040196 | tf_op jit(solution)/shard_map/while
  355.9 5.2 %copy-start = (f32[8,256,1792]{2,1,0:T(8,128)}, f32[8,256,1792]{2,1,0:T(8,128)S(1)}, u32[]{:S(2)}) copy-start(f32[8,256,1792]{2,1,0:T(8,128)S(1)} %get-tuple-element.165) | copy-start | bytes 44040196 | tf_op jit(solution)/shard_map/while
  381.6 5.2 %copy-start = (f32[8,256,1792]{2,1,0:T(8,128)}, f32[8,256,1792]{2,1,0:T(8,128)S(1)}, u32[]{:S(2)}) copy-start(f32[8,256,1792]{2,1,0:T(8,128)S(1)} %get-tuple-element.165) | copy-start | bytes 44040196 | tf_op jit(solution)/shard_map/while
Sparse Core Ops, SparseCore 0:
  51.2 123.3 all-gather.2
where the time goes:
time: 518 us; the launch traced here: 516 us
  waiting for transfers between devices  123 us (24%)
  matrix products  108 us (21%)
  blocking collectives  98.4 us (19%)
  local copies, waits for them, and re-layouts  88.7 us (17%)
  other arithmetic  45.5 us (9%)
  loops' own time  22.5 us (4%)
  between operations  17.9 us (3%)
  starting transfers between devices  12.6 us (2%)
    all_to_all x1, waiting for transfers between devices, per_device(): lax.all_to_all(outgoing, 'slot', split_axis=0, concat_axis=0, tiled=True)  122 us
    psum x1, blocking collectives, per_device(): lax.psum(deviation * deviation, ('prompt', 'slot'))  70.7 us
    dot_general x8, matrix products, one_group(): jnp.einsum('gsk,kd->gsd', rounded, value_rows, preferred_element_type=jnp...  57.3 us
    while x16, local copies, waits for them, and re-layouts  41.7 us
    dot_general x8, matrix products, one_group(): jnp.einsum('gsd,kd->gsk', query_rows, key_rows, preferred_element_type=jn...  34.5 us
    reduce_sum x8, other arithmetic, one_group(): totals = jnp.sum(weights, axis=-1, keepdims=True)  31.9 us
    psum x1, blocking collectives, per_device(): centre = lax.psum(score, 'slot') / slot_count  27.7 us
    another operation x1, loops' own time, per_device(): blocks = lax.map(one_group, jnp.arange(KVH, dtype=jnp.int32))  22.5 us
  transfers between devices with their start and end apart: 3, of which 1 were waited for; matrix products, arithmetic and copies ran while one was open for 8% of the time, Pallas kernels for 0%

commit v1 on v0

v1 whole, which is shorter than its diff:
```python
import math

import jax
import jax.numpy as jnp
from jax import lax
from jax.experimental import pallas as pl
from jax.experimental.pallas import tpu as pltpu
from jax.sharding import PartitionSpec as P

HEADS = 64
KVH = 8
HD = 128
GROUPS = HEADS // KVH
MESH = pl.DeviceIdType.MESH
OFFSETS = (
    (1, 0, 0), (3, 0, 0), (0, 1, 0), (2, 0, 0), (1, 1, 0),
    (3, 1, 0), (0, 1, 1), (2, 1, 0), (1, 0, 1), (3, 0, 1),
    (2, 0, 1), (1, 1, 1), (3, 1, 1), (2, 1, 1), (0, 0, 1),
)
NEG = -1e30


def pack_kernel(routes_ref, patch_ref, out_ref, live_ref):
    for g in range(KVH):
        out_ref[g, 0, :, :HD] = patch_ref[0, :, g * HD:(g + 1) * HD]
        out_ref[g, 0, :, HD:] = patch_ref[0, :, (KVH + g) * HD:(KVH + g + 1) * HD]

    @pl.when(pl.program_id(0) == 0)
    def _():
        lane = lax.broadcasted_iota(jnp.int32, live_ref.shape, 1)
        live = jnp.zeros(live_ref.shape, jnp.int32)
        for k in range(routes_ref.shape[1]):
            live = live + jnp.where(lane == routes_ref[0, k], 1, 0)
        live_ref[...] = live


def pack(routes, patch):
    slots, rows, width = patch.shape

    def source(d, routes_ref):
        slot = jnp.int32(0)
        for k in range(slots):
            slot = jnp.where(routes_ref[0, k] == d, jnp.int32(k), slot)
        return (slot, 0, 0)

    return pl.pallas_call(
        pack_kernel,
        grid_spec=pltpu.PrefetchScalarGridSpec(
            num_scalar_prefetch=1,
            grid=(slots,),
            in_specs=[pl.BlockSpec((1, rows, width), source)],
            out_specs=[
                pl.BlockSpec((KVH, 1, rows, 2 * HD), lambda d, r: (0, d, 0, 0)),
                pl.BlockSpec((8, 128), lambda d, r: (0, 0)),
            ],
        ),
        out_shape=[
            jax.ShapeDtypeStruct((KVH, slots, rows, 2 * HD), jnp.bfloat16),
            jax.ShapeDtypeStruct((8, 128), jnp.int32),
        ],
        name="pack",
    )(routes, patch)


def judge_kernel(
    plen_ref, live_ref, tiles_ref, prefix_ref, queries_ref, suffix_ref, head_ref,
    context_ref, advantage_ref,
    *scratch,
):
    image = scratch[:KVH]
    (
        prefix, suffix, queries, keys, values, context, acc,
        routes, routes_s, scores_out, scores_in, squares_out, squares_in,
        local_sem, own_sem, out_sem, tile_send, tile_recv,
        route_send, route_recv, prefix_send, prefix_recv, relay_sem,
        score_send, score_recv, square_send, square_recv,
    ) = scratch[KVH:]
    me = lax.axis_index("slot")
    prompt = lax.axis_index("prompt")
    n_slot = lax.axis_size("slot")
    n_prompt = lax.axis_size("prompt")
    x, y, c = me // 4, (me // 2) % 2, me % 2
    chip = me // 2
    n_rows = keys.shape[0]
    n_prefix = prefix.shape[2]
    n_suffix = suffix.shape[0]
    tile = image[0].shape[1]
    n_tiles = (n_rows - n_prefix - n_suffix) // tile

    def peer(offset):
        tx = lax.rem(x + offset[0], 4)
        ty = lax.rem(y + offset[1], 2)
        tc = lax.rem(c + offset[2], 2)
        return (tx * 2 + ty) * 2 + tc

    def remote(src, dst, send, recv, **where):
        return pltpu.make_async_remote_copy(
            src, dst, send, recv, device_id=where, device_id_type=MESH
        )

    load_queries = pltpu.make_async_copy(queries_ref, queries, local_sem.at[0])
    load_suffix = pltpu.make_async_copy(suffix_ref, suffix, local_sem.at[1])
    load_prefix = pltpu.make_async_copy(prefix_ref, prefix.at[c, chip], local_sem.at[2])
    load_routes = pltpu.make_async_copy(live_ref, routes.at[me], local_sem.at[3])
    load_prefix.start()
    load_routes.start()
    barrier = pltpu.get_barrier_semaphore()
    for k in range(1, n_slot):
        pl.semaphore_signal(
            barrier, inc=1, device_id={"slot": lax.rem(me + k, n_slot)}, device_id_type=MESH
        )
    for k in range(1, n_prompt):
        pl.semaphore_signal(
            barrier, inc=1, device_id={"prompt": lax.rem(prompt + k, n_prompt)},
            device_id_type=MESH,
        )
    pl.semaphore_wait(barrier, n_slot + n_prompt - 2)

    for offset in OFFSETS:
        remote(live_ref, routes.at[me], route_send, route_recv, slot=peer(offset)).start()
    for offset in OFFSETS:
        if offset[2] == 0:
            remote(
                prefix_ref, prefix.at[c, chip], prefix_send, prefix_recv, slot=peer(offset)
            ).start()
    for g in range(KVH):
        for offset in OFFSETS:
            target = peer(offset)
            remote(
                tiles_ref.at[g, target], image[g].at[me], tile_send.at[g], tile_recv.at[g],
                slot=target,
            ).start()
    load_suffix.start()
    load_queries.start()
    for g in range(KVH):
        pltpu.make_async_copy(tiles_ref.at[g, me], image[g].at[me], own_sem.at[g]).start()

    others = prefix.at[0, pl.ds(0, n_slot // 2 - 1)]
    load_prefix.wait()
    pltpu.make_async_copy(others, others, prefix_recv).wait()
    relay = remote(
        prefix.at[c], prefix.at[c], relay_sem.at[0], relay_sem.at[1], slot=me + 1 - 2 * c
    )
    relay.start()

    load_routes.wait()
    arrived = routes.at[pl.ds(0, n_slot - 1)]
    pltpu.make_async_copy(arrived, arrived, route_recv).wait()
    fetch = pltpu.make_async_copy(routes, routes_s, local_sem.at[3])
    fetch.start()
    fetch.wait()
    index = [jnp.int32(0)] * n_tiles
    count = jnp.int32(0)
    for s in range(n_slot):
        alive = routes_s[s, 0, me]
        for j in range(n_tiles):
            index[j] = jnp.where(
                jnp.logical_and(alive > 0, count == j), jnp.int32(s), index[j]
            )
        count = count + jnp.where(alive > 0, 1, 0)

    row = lax.broadcasted_iota(jnp.int32, (n_prefix, HD), 0)
    inside = row < plen_ref[0]
    values[:n_prefix, HD:] = jnp.where(inside, 1.0, 0.0).astype(jnp.bfloat16)
    values[n_prefix:, HD:] = jnp.ones((n_rows - n_prefix, HD), jnp.bfloat16)
    acc[...] = jnp.zeros_like(acc)
    load_suffix.wait()
    load_queries.wait()
    relay.wait()

    step = math.log2(math.e) / math.sqrt(HD)
    above = n_rows - n_suffix

    def one_group(g, carry):
        k_prefix = prefix[lax.rem(g, 2), g // 2].astype(jnp.float32)
        v_prefix = prefix[lax.rem(g, 2), KVH // 2 + g // 2].astype(jnp.float32)
        inside = lax.broadcasted_iota(jnp.int32, (n_prefix, HD), 0) < plen_ref[0]
        keys[:n_prefix, :] = jnp.where(inside, k_prefix, k_prefix[0:1, :]).astype(jnp.bfloat16)
        values[:n_prefix, :HD] = jnp.where(inside, v_prefix, 0.0).astype(jnp.bfloat16)
        k_at = pl.multiple_of(g * HD, HD)
        v_at = pl.multiple_of((KVH + g) * HD, HD)
        keys[above:, :] = suffix[:, pl.ds(k_at, HD)]
        values[above:, :HD] = suffix[:, pl.ds(v_at, HD)]
        for k in range(KVH):
            @pl.when(g == k)
            def _():
                landed = image[k].at[pl.ds(0, n_slot - 1)]
                pltpu.make_async_copy(landed, landed, tile_recv.at[k]).wait()
                pltpu.make_async_copy(
                    tiles_ref.at[k, me], image[k].at[me], own_sem.at[k]
                ).wait()
                for j in range(n_tiles):
                    at = n_prefix + j * tile
                    keys[at:at + tile, :] = image[k][index[j], :, :HD]
                    values[at:at + tile, :HD] = image[k][index[j], :, HD:]

        def one_head(i, carry):
            h = g * GROUPS + i
            at = pl.multiple_of(h * HD, HD)
            scores = lax.dot_general(
                queries[:, pl.ds(at, HD)], keys[...], (((1,), (1,)), ((), ())),
                preferred_element_type=jnp.float32,
            )
            seen = scores[:, :above]
            own = scores[:, above:]
            keep = lax.broadcasted_iota(jnp.int32, own.shape, 1) <= lax.broadcasted_iota(
                jnp.int32, own.shape, 0
            )
            own = jnp.where(keep, own, NEG)
            peak = jnp.maximum(
                jnp.max(seen, axis=1, keepdims=True), jnp.max(own, axis=1, keepdims=True)
            )
            w_seen = jnp.exp2((seen - peak) * step).astype(jnp.bfloat16)
            w_own = jnp.exp2((own - peak) * step).astype(jnp.bfloat16)
            mixed = jnp.dot(
                w_seen, values[:above, :], preferred_element_type=jnp.float32
            ) + jnp.dot(w_own, values[above:, :], preferred_element_type=jnp.float32)
            rounded = (mixed[:, :HD] / mixed[:, HD:]).astype(jnp.bfloat16)
            context[:, pl.ds(at, HD)] = rounded
            acc[...] += rounded[n_suffix - 8:, :].astype(jnp.float32) * head_ref[pl.ds(h, 1), :]
            return carry

        lax.fori_loop(0, GROUPS, one_head, 0)
        at = pl.multiple_of(g * GROUPS * HD, GROUPS * HD)
        block = pl.ds(at, GROUPS * HD)
        pltpu.make_async_copy(context.at[:, block], context_ref.at[:, block], out_sem).start()
        return carry

    lax.fori_loop(0, KVH, one_group, 0)

    score = jnp.sum(acc[7:8, :], axis=1, keepdims=True)
    score = jnp.broadcast_to(score, scores_out.shape)
    scores_out[...] = score
    for offset in OFFSETS:
        remote(scores_out, scores_in.at[me], score_send, score_recv, slot=peer(offset)).start()
    scores_in[me] = score
    arrived = scores_in.at[pl.ds(0, n_slot - 1)]
    pltpu.make_async_copy(arrived, arrived, score_recv).wait()
    centre = jnp.sum(scores_in[...], axis=0) / n_slot
    deviation = scores_in[...] - centre[None]
    squares = jnp.sum(deviation * deviation, axis=0)
    squares_out[...] = squares
    for k in range(1, n_prompt):
        remote(
            squares_out, squares_in.at[prompt], square_send, square_recv,
            prompt=lax.rem(prompt + k, n_prompt),
        ).start()
    squares_in[prompt] = squares
    arrived_p = squares_in.at[pl.ds(0, n_prompt - 1)]
    pltpu.make_async_copy(arrived_p, arrived_p, square_recv).wait()
    spread = jnp.sum(squares_in[...], axis=0) / (n_slot * n_prompt)
    result = (score - centre) / jnp.sqrt(spread + 1e-06)
    advantage_ref[...] = result[0:1, 0:1]

    pltpu.make_async_copy(arrived, arrived, score_send).wait()
    pltpu.make_async_copy(arrived_p, arrived_p, square_send).wait()
    sent = routes.at[pl.ds(0, n_slot - 1)]
    pltpu.make_async_copy(sent, sent, route_send).wait()
    pltpu.make_async_copy(others, others, prefix_send).wait()
    for k in range(KVH):
        landed = image[k].at[pl.ds(0, n_slot - 1)]
        pltpu.make_async_copy(landed, landed, tile_send.at[k]).wait()
    pltpu.make_async_copy(context, context_ref, out_sem).wait()


def judge(plen, live, tiles, prefix, queries, suffix, head):
    groups, n_slot, tile, width = tiles.shape
    n_suffix, q_width = queries.shape
    n_prefix = prefix.shape[0]
    n_rows = n_prefix + n_slot // 2 * tile + n_suffix
    n_prompt = lax.axis_size("prompt")
    vmem = pl.BlockSpec(memory_space=pltpu.VMEM)
    hbm = pl.BlockSpec(memory_space=pl.ANY)
    dma = pltpu.SemaphoreType.DMA
    return pl.pallas_call(
        judge_kernel,
        in_specs=[
            pl.BlockSpec(memory_space=pltpu.SMEM), vmem, hbm, hbm, hbm, hbm, vmem,
        ],
        out_specs=[hbm, vmem],
        out_shape=[
            jax.ShapeDtypeStruct((n_suffix, q_width), jnp.bfloat16),
            jax.ShapeDtypeStruct((1, 1), jnp.float32),
        ],
        scratch_shapes=[pltpu.VMEM((n_slot, tile, width), jnp.bfloat16)] * groups + [
            pltpu.VMEM((2, n_slot // 2, n_prefix, HD), jnp.bfloat16),
            pltpu.VMEM(suffix.shape, jnp.bfloat16),
            pltpu.VMEM(queries.shape, jnp.bfloat16),
            pltpu.VMEM((n_rows, HD), jnp.bfloat16),
            pltpu.VMEM((n_rows, 2 * HD), jnp.bfloat16),
            pltpu.VMEM(queries.shape, jnp.bfloat16),
            pltpu.VMEM((8, HD), jnp.float32),
            pltpu.VMEM((n_slot, 8, 128), jnp.int32),
            pltpu.SMEM((n_slot, 8, 128), jnp.int32),
            pltpu.VMEM((8, 128), jnp.float32),
            pltpu.VMEM((n_slot, 8, 128), jnp.float32),
            pltpu.VMEM((8, 128), jnp.float32),
            pltpu.VMEM((n_prompt, 8, 128), jnp.float32),
            dma((4,)), dma((groups,)), dma(()), dma((groups,)), dma((groups,)),
            dma(()), dma(()), dma(()), dma(()), dma((2,)),
            dma(()), dma(()), dma(()), dma(()),
        ],
        compiler_params=pltpu.CompilerParams(
            collective_id=0, has_side_effects=True, vmem_limit_bytes=56 << 20
        ),
        name="judge",
    )(plen, live, tiles, prefix, queries, suffix, head)


def per_device(patch_kv, routes, prefix_kv, prefix_len, queries, suffix_kv, score_head):
    tiles, live = pack(routes, patch_kv[0])
    context, advantage = judge(
        prefix_len, live, tiles, prefix_kv[0], queries[0, 0], suffix_kv[0, 0],
        score_head.reshape(HEADS, HD),
    )
    return (context[None, None], advantage)


def solution(mesh):
    placed = (
        P("prompt", "slot", None, None),
        P("prompt", "slot"),
        P("prompt", None, "slot"),
        P("prompt"),
        P("prompt", "slot", None, None),
        P("prompt", "slot", None, None),
        P(),
    )
    return jax.shard_map(
        per_device,
        mesh=mesh,
        in_specs=placed,
        out_specs=(P("prompt", "slot", None, None), P("prompt", "slot")),
        check_vma=False,
    )
```

time: 518 us -> 157 us (0.30)
  Pallas kernels: 0 us -> 149 us
  waiting for transfers between devices: 123 us -> 0 us
  matrix products: 108 us -> 0 us
  blocking collectives: 98.4 us -> 0 us
  local copies, waits for them, and re-layouts: 88.7 us -> 4.64 us
  other arithmetic: 45.5 us -> 0 us
  loops' own time: 22.5 us -> 0 us
  between operations: 17.9 us -> 3.04 us
  starting transfers between devices: 12.6 us -> 0 us
    pallas_call x0 -> x2, Pallas kernels: none -> 149 us  [the longest x1 137 us: judge(): pl.pallas_call(judge_kernel, in_specs=[pl.BlockSpec(memory_space=pltpu.SM...]
    all_to_all x2 -> x0, waiting for transfers between devices: 122 us -> none  [the longest x1 122 us: per_device(): lax.all_to_all(outgoing, 'slot', split_axis=0, concat_axis=0, tiled=True)]
    dot_general x17 -> x0, matrix products: 108 us -> none  [the longest x8 57.3 us: one_group(): jnp.einsum('gsk,kd->gsd', rounded, value_rows, preferred_element_type=jnp...]
    psum x2 -> x0, blocking collectives: 98.4 us -> none  [the longest x1 70.7 us: per_device(): lax.psum(deviation * deviation, ('prompt', 'slot'))]
    while x16 -> x0, local copies, waits for them, and re-layouts: 41.7 us -> none
    reduce_sum x9 -> x0, other arithmetic: 32.5 us -> none  [the longest x8 31.9 us: one_group(): totals = jnp.sum(weights, axis=-1, keepdims=True)]
    another operation x1 -> x0, loops' own time: 22.5 us -> none  [per_device(): blocks = lax.map(one_group, jnp.arange(KVH, dtype=jnp.int32))]
    convert_element_type x3 -> x0, local copies, waits for them, and re-layouts: 19.4 us -> none  [the longest x1 11.4 us: per_device(): outgoing = jnp.einsum('dk,krc->drc', matches.astype(jnp.bfloat16), patch_...]
  transfers between devices with their start and end apart: 3 -> 0, of which waited for: 1 -> 0; matrix products, arithmetic and copies ran while one was open for 8% -> 0% of each run, Pallas kernels for 0% -> 0%
where the time goes in v1:
time: 157 us; the launch traced here: 156 us
  Pallas kernels  149 us (95%)
  local copies, waits for them, and re-layouts  4.64 us (3%)
  between operations  3.04 us (2%)
    pallas_call x1, Pallas kernels, judge(): pl.pallas_call(judge_kernel, in_specs=[pl.BlockSpec(memory_space=pltpu.SM...  137 us
    pallas_call x1, Pallas kernels, pack(): pl.pallas_call(pack_kernel, grid_spec=pltpu.PrefetchScalarGridSpec(num_sc...  12.1 us
    unnamed x1, local copies, waits for them, and re-layouts  4.64 us

profile of v1, /device:TPU:1, one launch (start us, length us, event | category | flops | bytes accessed | tf_op | source)
XLA Modules:
  0.0 156.3 jit_solution(1606533651670850324)
XLA Ops:
  1.3 12.1 %pack.1 = (bf16[8,16,128,256]{3,2,1,0:T(8,128)(2,1)}, s32[8,128]{1,0:T(8,128)}) custom-call(s32[1,16]{1,0:T(1,128)} %routes_ref.1, bf16[16,128,2048]{2,1,0:T(8,128)(2,1)} %bitcast.6), custom_call_target="tpu_custom_call" | custom-call | tf_op jit(solution)/shard_map/pack/pallas_call | solution.py:46
  13.4 136.5 %judge.1 = (bf16[256,8192]{1,0:T(8,128)(2,1)}, f32[1,1]{1,0:T(1,128)}) custom-call(s32[1]{0:T(128)S(6)} %copy.11.plen_ref, s32[8,128]{1,0:T(8,128)} %get-tuple-element.6.live_ref, bf16[8,16,128,256]{3,2,1,0:T(8,128)(2,1)} %get-tuple-element.7.tiles_ref, bf16[512,128]{1,0:T(8,128)(2,1)} %bitcast.10, bf16[256,8192]{1,0:T(8,128)(2,1)} %bitcast.7, ...), custom_call_target="tpu_custom_call" | custom-call | tf_op jit(solution)/shard_map/judge/pallas_call | solution.py:275
  149.9 4.6 %copy.12 = bf16[1,1,256,8192]{3,2,1,0:T(8,128)(2,1)} copy(bf16[1,1,256,8192]{3,2,1,0:T(8,128)(2,1)} %bitcast.8) | data formatting | bytes 8388608

commit v2 on v1

v2 whole, which is shorter than its diff:
```python
import math

import jax
import jax.numpy as jnp
from jax import lax
from jax.experimental import pallas as pl
from jax.experimental.pallas import tpu as pltpu
from jax.sharding import PartitionSpec as P

HEADS = 64
KVH = 8
HD = 128
GROUPS = HEADS // KVH
MESH = pl.DeviceIdType.MESH
OFFSETS = (
    (1, 0, 0), (3, 0, 0), (0, 1, 0), (2, 0, 0), (1, 1, 0),
    (3, 1, 0), (0, 1, 1), (2, 1, 0), (1, 0, 1), (3, 0, 1),
    (2, 0, 1), (1, 1, 1), (3, 1, 1), (2, 1, 1), (0, 0, 1),
)
NEG = -1e30


def judge_kernel(
    plen_ref, routes_ref, patch_ref, prefix_ref, queries_ref, suffix_ref, head_ref,
    context_ref, advantage_ref,
    *scratch,
):
    image = scratch[:KVH]
    staged = scratch[KVH:2 * KVH]
    packed = scratch[2 * KVH:3 * KVH]
    (
        prefix, suffix, queries, keys, values, context, scores_a, scores_b, acc,
        live, routes, routes_s, scores_out, scores_in, squares_out, squares_in,
        local_sem, stage_sem, out_sem, tile_send, tile_recv,
        route_send, route_recv, prefix_send, prefix_recv, relay_sem,
        score_send, score_recv, square_send, square_recv,
    ) = scratch[3 * KVH:]
    me = lax.axis_index("slot")
    prompt = lax.axis_index("prompt")
    n_slot = lax.axis_size("slot")
    n_prompt = lax.axis_size("prompt")
    x, y, c = me // 4, (me // 2) % 2, me % 2
    chip = me // 2
    n_rows = keys.shape[0]
    n_prefix = prefix.shape[2]
    n_suffix = suffix.shape[0]
    tile = image[0].shape[1]
    n_tiles = (n_rows - n_prefix - n_suffix) // tile

    def peer(offset):
        tx = lax.rem(x + offset[0], 4)
        ty = lax.rem(y + offset[1], 2)
        tc = lax.rem(c + offset[2], 2)
        return (tx * 2 + ty) * 2 + tc

    def remote(src, dst, send, recv, **where):
        return pltpu.make_async_remote_copy(
            src, dst, send, recv, device_id=where, device_id_type=MESH
        )

    def stage(g):
        return [
            pltpu.make_async_copy(
                patch_ref.at[:, :, pl.ds(at * HD, HD)], staged[g].at[:, :, pl.ds(k * HD, HD)],
                stage_sem.at[g],
            )
            for k, at in enumerate((g, KVH + g))
        ]

    load_queries = pltpu.make_async_copy(queries_ref, queries, local_sem.at[0])
    load_suffix = pltpu.make_async_copy(suffix_ref, suffix, local_sem.at[1])
    load_prefix = pltpu.make_async_copy(prefix_ref, prefix.at[c, chip], local_sem.at[2])
    for g in range(KVH):
        for copy in stage(g):
            copy.start()
    load_prefix.start()
    barrier = pltpu.get_barrier_semaphore()
    for k in range(1, n_slot):
        pl.semaphore_signal(
            barrier, inc=1, device_id={"slot": lax.rem(me + k, n_slot)}, device_id_type=MESH
        )
    for k in range(1, n_prompt):
        pl.semaphore_signal(
            barrier, inc=1, device_id={"prompt": lax.rem(prompt + k, n_prompt)},
            device_id_type=MESH,
        )
    lane = lax.broadcasted_iota(jnp.int32, live.shape, 1)
    flags = jnp.zeros(live.shape, jnp.int32)
    slots = [jnp.int32(0)] * n_slot
    own_slot = jnp.int32(0)
    for k in range(n_slot):
        judge_of = routes_ref[0, k]
        flags = flags + jnp.where(lane == judge_of, 1, 0)
        own_slot = jnp.where(judge_of == me, jnp.int32(k), own_slot)
        for d in range(n_slot):
            slots[d] = jnp.where(judge_of == d, jnp.int32(k), slots[d])
    live[...] = flags
    routes[me] = flags
    pl.semaphore_wait(barrier, n_slot + n_prompt - 2)

    for offset in OFFSETS:
        if offset[2] == 0:
            remote(
                prefix_ref, prefix.at[c, chip], prefix_send, prefix_recv, slot=peer(offset)
            ).start()
    for offset in OFFSETS:
        remote(live, routes.at[me], route_send, route_recv, slot=peer(offset)).start()

    def send_tiles(g):
        for offset in OFFSETS:
            target = peer(offset)
            remote(
                packed[g].at[target], image[g].at[me], tile_send.at[g], tile_recv.at[g],
                slot=target,
            ).start()

    for g in range(KVH):
        for copy in stage(g):
            copy.wait()
        for d in range(n_slot):
            packed[g][d] = staged[g][slots[d]]
        image[g][me] = staged[g][own_slot]
        if g > 0:
            send_tiles(g - 1)
    send_tiles(KVH - 1)
    load_suffix.start()
    load_queries.start()

    others = prefix.at[0, pl.ds(0, n_slot // 2 - 1)]
    load_prefix.wait()
    pltpu.make_async_copy(others, others, prefix_recv).wait()
    relay = remote(
        prefix.at[c], prefix.at[c], relay_sem.at[0], relay_sem.at[1], slot=me + 1 - 2 * c
    )
    relay.start()

    arrived = routes.at[pl.ds(0, n_slot - 1)]
    pltpu.make_async_copy(arrived, arrived, route_recv).wait()
    fetch = pltpu.make_async_copy(routes, routes_s, local_sem.at[3])
    fetch.start()
    fetch.wait()
    index = [jnp.int32(0)] * n_tiles
    count = jnp.int32(0)
    for s in range(n_slot):
        alive = routes_s[s, 0, me]
        for j in range(n_tiles):
            index[j] = jnp.where(
                jnp.logical_and(alive > 0, count == j), jnp.int32(s), index[j]
            )
        count = count + jnp.where(alive > 0, 1, 0)

    inside = lax.broadcasted_iota(jnp.int32, (16, n_prefix), 1) < plen_ref[0]
    values[HD:, :n_prefix] = jnp.where(inside, 1.0, 0.0).astype(jnp.bfloat16)
    values[HD:, n_prefix:] = jnp.ones((16, n_rows - n_prefix), jnp.bfloat16)
    acc[...] = jnp.zeros_like(acc)
    load_suffix.wait()
    load_queries.wait()
    relay.wait()

    step = math.log2(math.e) / math.sqrt(HD)
    above = n_rows - n_suffix

    def score_head(scores, h):
        at = pl.multiple_of(h * HD, HD)
        scores[...] = lax.dot_general(
            keys[...], queries[:, pl.ds(at, HD)], (((1,), (1,)), ((), ())),
            preferred_element_type=jnp.float32,
        )

    def mix_head(scores, h):
        seen = scores[:above, :]
        own = scores[above:, :]
        keep = lax.broadcasted_iota(jnp.int32, own.shape, 0) <= lax.broadcasted_iota(
            jnp.int32, own.shape, 1
        )
        own = jnp.where(keep, own, NEG)
        peak = jnp.maximum(
            jnp.max(seen, axis=0, keepdims=True), jnp.max(own, axis=0, keepdims=True)
        )
        w_seen = jnp.exp2((seen - peak) * step).astype(jnp.bfloat16)
        w_own = jnp.exp2((own - peak) * step).astype(jnp.bfloat16)
        weights = jnp.concatenate([w_seen, w_own], axis=0)
        mixed = jnp.dot(values[...], weights, preferred_element_type=jnp.float32)
        rounded = (mixed[:HD] / mixed[HD:HD + 1]).T.astype(jnp.bfloat16)
        at = pl.multiple_of(h * HD, HD)
        context[:, pl.ds(at, HD)] = rounded
        acc[...] += rounded[n_suffix - 8:, :].astype(jnp.float32) * head_ref[pl.ds(h, 1), :]

    def one_group(g, carry):
        k_prefix = prefix[lax.rem(g, 2), g // 2].astype(jnp.float32)
        v_prefix = prefix[lax.rem(g, 2), KVH // 2 + g // 2].astype(jnp.float32)
        inside = lax.broadcasted_iota(jnp.int32, (n_prefix, HD), 0) < plen_ref[0]
        keys[:n_prefix, :] = jnp.where(inside, k_prefix, k_prefix[0:1, :]).astype(jnp.bfloat16)
        values[:HD, :n_prefix] = jnp.where(inside, v_prefix, 0.0).T.astype(jnp.bfloat16)
        k_at = pl.multiple_of(g * HD, HD)
        v_at = pl.multiple_of((KVH + g) * HD, HD)
        keys[above:, :] = suffix[:, pl.ds(k_at, HD)]
        values[:HD, above:] = suffix[:, pl.ds(v_at, HD)].T
        for k in range(KVH):
            @pl.when(g == k)
            def _():
                landed = image[k].at[pl.ds(0, n_slot - 1)]
                pltpu.make_async_copy(landed, landed, tile_recv.at[k]).wait()
                for j in range(n_tiles):
                    at = n_prefix + j * tile
                    keys[at:at + tile, :] = image[k][index[j], :, :HD]
                    values[:HD, at:at + tile] = image[k][index[j], :, HD:].T

        first = g * GROUPS
        last = first + GROUPS - 1
        score_head(scores_a, first)

        def two_heads(i, carry):
            h = first + 2 * i
            score_head(scores_b, h + 1)
            mix_head(scores_a, h)
            score_head(scores_a, jnp.minimum(h + 2, last))
            mix_head(scores_b, h + 1)
            return carry

        lax.fori_loop(0, GROUPS // 2, two_heads, 0)
        at = pl.multiple_of(g * GROUPS * HD, GROUPS * HD)
        block = pl.ds(at, GROUPS * HD)
        pltpu.make_async_copy(context.at[:, block], context_ref.at[:, block], out_sem).start()
        return carry

    lax.fori_loop(0, KVH, one_group, 0)

    score = jnp.sum(acc[7:8, :], axis=1, keepdims=True)
    score = jnp.broadcast_to(score, scores_out.shape)
    scores_out[...] = score
    for offset in OFFSETS:
        remote(scores_out, scores_in.at[me], score_send, score_recv, slot=peer(offset)).start()
    scores_in[me] = score
    arrived = scores_in.at[pl.ds(0, n_slot - 1)]
    pltpu.make_async_copy(arrived, arrived, score_recv).wait()
    centre = jnp.sum(scores_in[...], axis=0) / n_slot
    deviation = scores_in[...] - centre[None]
    squares = jnp.sum(deviation * deviation, axis=0)
    squares_out[...] = squares
    for k in range(1, n_prompt):
        remote(
            squares_out, squares_in.at[prompt], square_send, square_recv,
            prompt=lax.rem(prompt + k, n_prompt),
        ).start()
    squares_in[prompt] = squares
    arrived_p = squares_in.at[pl.ds(0, n_prompt - 1)]
    pltpu.make_async_copy(arrived_p, arrived_p, square_recv).wait()
    spread = jnp.sum(squares_in[...], axis=0) / (n_slot * n_prompt)
    result = (score - centre) / jnp.sqrt(spread + 1e-06)
    advantage_ref[...] = result[0:1, 0:1]

    pltpu.make_async_copy(arrived, arrived, score_send).wait()
    pltpu.make_async_copy(arrived_p, arrived_p, square_send).wait()
    sent = routes.at[pl.ds(0, n_slot - 1)]
    pltpu.make_async_copy(sent, sent, route_send).wait()
    pltpu.make_async_copy(others, others, prefix_send).wait()
    for k in range(KVH):
        landed = image[k].at[pl.ds(0, n_slot - 1)]
        pltpu.make_async_copy(landed, landed, tile_send.at[k]).wait()
    pltpu.make_async_copy(context, context_ref, out_sem).wait()


def judge(plen, routes, patch, prefix, queries, suffix, head):
    n_slot, tile, width = patch.shape
    n_suffix, q_width = queries.shape
    n_prefix = prefix.shape[0]
    n_rows = n_prefix + n_slot // 2 * tile + n_suffix
    n_prompt = lax.axis_size("prompt")
    vmem = pl.BlockSpec(memory_space=pltpu.VMEM)
    smem = pl.BlockSpec(memory_space=pltpu.SMEM)
    hbm = pl.BlockSpec(memory_space=pl.ANY)
    dma = pltpu.SemaphoreType.DMA
    return pl.pallas_call(
        judge_kernel,
        in_specs=[smem, smem, hbm, hbm, hbm, hbm, vmem],
        out_specs=[hbm, vmem],
        out_shape=[
            jax.ShapeDtypeStruct((n_suffix, q_width), jnp.bfloat16),
            jax.ShapeDtypeStruct((1, 1), jnp.float32),
        ],
        scratch_shapes=[pltpu.VMEM((n_slot, tile, 2 * HD), jnp.bfloat16)] * (3 * KVH) + [
            pltpu.VMEM((2, n_slot // 2, n_prefix, HD), jnp.bfloat16),
            pltpu.VMEM(suffix.shape, jnp.bfloat16),
            pltpu.VMEM(queries.shape, jnp.bfloat16),
            pltpu.VMEM((n_rows, HD), jnp.bfloat16),
            pltpu.VMEM((HD + 16, n_rows), jnp.bfloat16),
            pltpu.VMEM(queries.shape, jnp.bfloat16),
            pltpu.VMEM((n_rows, n_suffix), jnp.float32),
            pltpu.VMEM((n_rows, n_suffix), jnp.float32),
            pltpu.VMEM((8, HD), jnp.float32),
            pltpu.VMEM((8, 128), jnp.int32),
            pltpu.VMEM((n_slot, 8, 128), jnp.int32),
            pltpu.SMEM((n_slot, 8, 128), jnp.int32),
            pltpu.VMEM((8, 128), jnp.float32),
            pltpu.VMEM((n_slot, 8, 128), jnp.float32),
            pltpu.VMEM((8, 128), jnp.float32),
            pltpu.VMEM((n_prompt, 8, 128), jnp.float32),
            dma((4,)), dma((KVH,)), dma(()), dma((KVH,)), dma((KVH,)),
            dma(()), dma(()), dma(()), dma(()), dma((2,)),
            dma(()), dma(()), dma(()), dma(()),
        ],
        compiler_params=pltpu.CompilerParams(
            collective_id=0, has_side_effects=True, vmem_limit_bytes=58 << 20
        ),
        name="judge",
    )(plen, routes, patch, prefix, queries, suffix, head)


def per_device(patch_kv, routes, prefix_kv, prefix_len, queries, suffix_kv, score_head):
    context, advantage = judge(
        prefix_len, routes, patch_kv[0], prefix_kv[0], queries[0, 0], suffix_kv[0, 0],
        score_head.reshape(HEADS, HD),
    )
    return (context[None, None], advantage)


def solution(mesh):
    placed = (
        P("prompt", "slot", None, None),
        P("prompt", "slot"),
        P("prompt", None, "slot"),
        P("prompt"),
        P("prompt", "slot", None, None),
        P("prompt", "slot", None, None),
        P(),
    )
    return jax.shard_map(
        per_device,
        mesh=mesh,
        in_specs=placed,
        out_specs=(P("prompt", "slot", None, None), P("prompt", "slot")),
        check_vma=False,
    )
```

time: 157 us -> 138 us (0.88)
  Pallas kernels: 149 us -> 131 us
    pallas_call x2 -> x1, Pallas kernels: 149 us -> 131 us  [judge(): pl.pallas_call(judge_kernel, in_specs=[smem, smem, hbm, hbm, hbm, hbm, vm...]
where the time goes in v2:
time: 138 us
  Pallas kernels  131 us (95%)
  local copies, waits for them, and re-layouts  4.64 us (3%)
  between operations  3.02 us (2%)
    pallas_call x1, Pallas kernels, judge(): pl.pallas_call(judge_kernel, in_specs=[smem, smem, hbm, hbm, hbm, hbm, vm...  131 us
    unnamed x1, local copies, waits for them, and re-layouts  4.64 us

profile of v2, /device:TPU:1, one launch (start us, length us, event | category | flops | bytes accessed | tf_op | source)
XLA Modules:
  0.0 138.2 jit_solution(1578102573063655152)
XLA Ops:
  1.3 130.6 %judge.1 = (bf16[256,8192]{1,0:T(8,128)(2,1)}, f32[1,1]{1,0:T(1,128)}) custom-call(s32[1]{0:T(128)S(6)} %copy.11.plen_ref, s32[1,16]{1,0:T(1,128)} %routes_ref.1, bf16[16,128,2048]{2,1,0:T(8,128)(2,1)} %bitcast.6, bf16[512,128]{1,0:T(8,128)(2,1)} %bitcast.10, bf16[256,8192]{1,0:T(8,128)(2,1)} %bitcast.7, bf16[256,2048]{1,0:T(8,128)(2,1)} %bitcast.9, ...), custom_call_target="tpu_custom_call" | custom-call | tf_op jit(solution)/shard_map/judge/pallas_call | solution.py:274
  131.9 4.6 %copy.12 = bf16[1,1,256,8192]{3,2,1,0:T(8,128)(2,1)} copy(bf16[1,1,256,8192]{3,2,1,0:T(8,128)(2,1)} %bitcast.8) | data formatting | bytes 8388608

commit v3 on v2

--- a/solution.py
+++ b/solution.py
@@ -22,16 +22,16 @@
 
 def judge_kernel(
     plen_ref, routes_ref, patch_ref, prefix_ref, queries_ref, suffix_ref, head_ref,
-    context_ref, advantage_ref,
+    context, advantage_ref,
     *scratch,
 ):
     image = scratch[:KVH]
     staged = scratch[KVH:2 * KVH]
     packed = scratch[2 * KVH:3 * KVH]
     (
-        prefix, suffix, queries, keys, values, context, scores_a, scores_b, acc,
+        prefix, suffix, queries, keys, values, scores_a, scores_b, acc,
         live, routes, routes_s, scores_out, scores_in, squares_out, squares_in,
-        local_sem, stage_sem, out_sem, tile_send, tile_recv,
+        local_sem, stage_sem, tile_send, tile_recv,
         route_send, route_recv, prefix_send, prefix_recv, relay_sem,
         score_send, score_recv, square_send, square_recv,
     ) = scratch[3 * KVH:]
@@ -70,9 +70,8 @@
     load_queries = pltpu.make_async_copy(queries_ref, queries, local_sem.at[0])
     load_suffix = pltpu.make_async_copy(suffix_ref, suffix, local_sem.at[1])
     load_prefix = pltpu.make_async_copy(prefix_ref, prefix.at[c, chip], local_sem.at[2])
-    for g in range(KVH):
-        for copy in stage(g):
-            copy.start()
+    for copy in stage(0) + stage(1):
+        copy.start()
     load_prefix.start()
     barrier = pltpu.get_barrier_semaphore()
     for k in range(1, n_slot):
@@ -117,6 +116,9 @@
     for g in range(KVH):
         for copy in stage(g):
             copy.wait()
+        if g + 2 < KVH:
+            for copy in stage(g + 2):
+                copy.start()
         for d in range(n_slot):
             packed[g][d] = staged[g][slots[d]]
         image[g][me] = staged[g][own_slot]
@@ -160,6 +162,27 @@
     step = math.log2(math.e) / math.sqrt(HD)
     above = n_rows - n_suffix
 
+    def add_score(rows, h):
+        acc[...] += rows.astype(jnp.float32) * head_ref[pl.ds(h, 1), :]
+
+    def score_last_rows(first):
+        tail = jnp.concatenate(
+            [
+                queries[n_suffix - 16:, (first + i) * HD:(first + i + 1) * HD]
+                for i in range(GROUPS)
+            ],
+            axis=0,
+        )
+        scores = lax.dot_general(
+            keys[...], tail, (((1,), (1,)), ((), ())), preferred_element_type=jnp.float32
+        )
+        peak = jnp.max(scores, axis=0, keepdims=True)
+        weights = jnp.exp2((scores - peak) * step).astype(jnp.bfloat16)
+        mixed = jnp.dot(values[...], weights, preferred_element_type=jnp.float32)
+        rounded = (mixed[:HD] / mixed[HD:HD + 1]).T.astype(jnp.bfloat16)
+        for i in range(GROUPS):
+            add_score(rounded[16 * i + 8:16 * i + 16, :], first + i)
+
     def score_head(scores, h):
         at = pl.multiple_of(h * HD, HD)
         scores[...] = lax.dot_general(
@@ -167,7 +190,7 @@
             preferred_element_type=jnp.float32,
         )
 
-    def mix_head(scores, h):
+    def mix_head(scores, h, score):
         seen = scores[:above, :]
         own = scores[above:, :]
         keep = lax.broadcasted_iota(jnp.int32, own.shape, 0) <= lax.broadcasted_iota(
@@ -184,9 +207,10 @@
         rounded = (mixed[:HD] / mixed[HD:HD + 1]).T.astype(jnp.bfloat16)
         at = pl.multiple_of(h * HD, HD)
         context[:, pl.ds(at, HD)] = rounded
-        acc[...] += rounded[n_suffix - 8:, :].astype(jnp.float32) * head_ref[pl.ds(h, 1), :]
-
-    def one_group(g, carry):
+        if score:
+            add_score(rounded[n_suffix - 8:, :], h)
+
+    def build(g, pieces):
         k_prefix = prefix[lax.rem(g, 2), g // 2].astype(jnp.float32)
         v_prefix = prefix[lax.rem(g, 2), KVH // 2 + g // 2].astype(jnp.float32)
         inside = lax.broadcasted_iota(jnp.int32, (n_prefix, HD), 0) < plen_ref[0]
@@ -196,7 +220,7 @@
         v_at = pl.multiple_of((KVH + g) * HD, HD)
         keys[above:, :] = suffix[:, pl.ds(k_at, HD)]
         values[:HD, above:] = suffix[:, pl.ds(v_at, HD)].T
-        for k in range(KVH):
+        for k in pieces:
             @pl.when(g == k)
             def _():
                 landed = image[k].at[pl.ds(0, n_slot - 1)]
@@ -206,32 +230,45 @@
                     keys[at:at + tile, :] = image[k][index[j], :, :HD]
                     values[:HD, at:at + tile] = image[k][index[j], :, HD:].T
 
+
+    def two_heads(first, i, score):
+        last = first + GROUPS - 1
+        h = first + 2 * i
+        score_head(scores_b, h + 1)
+        mix_head(scores_a, h, score)
+        score_head(scores_a, jnp.minimum(h + 2, last))
+        mix_head(scores_b, h + 1, score)
+
+    def one_group(g, carry):
+        build(g, range(KVH - 1))
         first = g * GROUPS
-        last = first + GROUPS - 1
         score_head(scores_a, first)
 
-        def two_heads(i, carry):
-            h = first + 2 * i
-            score_head(scores_b, h + 1)
-            mix_head(scores_a, h)
-            score_head(scores_a, jnp.minimum(h + 2, last))
-            mix_head(scores_b, h + 1)
+        def body(i, carry):
+            two_heads(first, i, True)
             return carry
 
-        lax.fori_loop(0, GROUPS // 2, two_heads, 0)
-        at = pl.multiple_of(g * GROUPS * HD, GROUPS * HD)
-        block = pl.ds(at, GROUPS * HD)
-        pltpu.make_async_copy(context.at[:, block], context_ref.at[:, block], out_sem).start()
+        lax.fori_loop(0, GROUPS // 2, body, 0)
         return carry
 
-    lax.fori_loop(0, KVH, one_group, 0)
-
+    lax.fori_loop(0, KVH - 1, one_group, 0)
+
+    final = KVH - 1
+    build(final, [final])
+    score_last_rows(final * GROUPS)
     score = jnp.sum(acc[7:8, :], axis=1, keepdims=True)
     score = jnp.broadcast_to(score, scores_out.shape)
     scores_out[...] = score
     for offset in OFFSETS:
         remote(scores_out, scores_in.at[me], score_send, score_recv, slot=peer(offset)).start()
     scores_in[me] = score
+    score_head(scores_a, final * GROUPS)
+
+    def early(i, carry):
+        two_heads(final * GROUPS, i, False)
+        return carry
+
+    lax.fori_loop(0, GROUPS // 4, early, 0)
     arrived = scores_in.at[pl.ds(0, n_slot - 1)]
     pltpu.make_async_copy(arrived, arrived, score_recv).wait()
     centre = jnp.sum(scores_in[...], axis=0) / n_slot
@@ -244,6 +281,7 @@
             prompt=lax.rem(prompt + k, n_prompt),
         ).start()
     squares_in[prompt] = squares
+    lax.fori_loop(GROUPS // 4, GROUPS // 2, early, 0)
     arrived_p = squares_in.at[pl.ds(0, n_prompt - 1)]
     pltpu.make_async_copy(arrived_p, arrived_p, square_recv).wait()
     spread = jnp.sum(squares_in[...], axis=0) / (n_slot * n_prompt)
@@ -258,7 +296,6 @@
     for k in range(KVH):
         landed = image[k].at[pl.ds(0, n_slot - 1)]
         pltpu.make_async_copy(landed, landed, tile_send.at[k]).wait()
-    pltpu.make_async_copy(context, context_ref, out_sem).wait()
 
 
 def judge(plen, routes, patch, prefix, queries, suffix, head):
@@ -274,9 +311,9 @@
     return pl.pallas_call(
         judge_kernel,
         in_specs=[smem, smem, hbm, hbm, hbm, hbm, vmem],
-        out_specs=[hbm, vmem],
+        out_specs=[vmem, vmem],
         out_shape=[
-            jax.ShapeDtypeStruct((n_suffix, q_width), jnp.bfloat16),
+            pltpu.VMEM((n_suffix, q_width), jnp.bfloat16),
             jax.ShapeDtypeStruct((1, 1), jnp.float32),
         ],
         scratch_shapes=[pltpu.VMEM((n_slot, tile, 2 * HD), jnp.bfloat16)] * (3 * KVH) + [
@@ -285,7 +322,6 @@
             pltpu.VMEM(queries.shape, jnp.bfloat16),
             pltpu.VMEM((n_rows, HD), jnp.bfloat16),
             pltpu.VMEM((HD + 16, n_rows), jnp.bfloat16),
-            pltpu.VMEM(queries.shape, jnp.bfloat16),
             pltpu.VMEM((n_rows, n_suffix), jnp.float32),
             pltpu.VMEM((n_rows, n_suffix), jnp.float32),
             pltpu.VMEM((8, HD), jnp.float32),
@@ -296,12 +332,12 @@
             pltpu.VMEM((n_slot, 8, 128), jnp.float32),
             pltpu.VMEM((8, 128), jnp.float32),
             pltpu.VMEM((n_prompt, 8, 128), jnp.float32),
-            dma((4,)), dma((KVH,)), dma(()), dma((KVH,)), dma((KVH,)),
+            dma((4,)), dma((KVH,)), dma((KVH,)), dma((KVH,)),
             dma(()), dma(()), dma(()), dma(()), dma((2,)),
             dma(()), dma(()), dma(()), dma(()),
         ],
         compiler_params=pltpu.CompilerParams(
-            collective_id=0, has_side_effects=True, vmem_limit_bytes=58 << 20
+            collective_id=0, has_side_effects=True, vmem_limit_bytes=52 << 20
         ),
         name="judge",
     )(plen, routes, patch, prefix, queries, suffix, head)

time: 138 us -> 130 us (0.942)
  Pallas kernels: 131 us -> 125 us
  local copies, waits for them, and re-layouts: 4.64 us -> 2.02 us
    pallas_call x1, Pallas kernels: 131 us -> 125 us  [judge(): pl.pallas_call(judge_kernel, in_specs=[smem, smem, hbm, hbm, hbm, hbm, vm...]
    unnamed x1, local copies, waits for them, and re-layouts: 4.64 us -> 2.02 us
where the time goes in v3:
time: 130 us
  Pallas kernels  125 us (96%)
  between operations  2.97 us (2%)
  local copies, waits for them, and re-layouts  2.02 us (2%)
    pallas_call x1, Pallas kernels, judge(): pl.pallas_call(judge_kernel, in_specs=[smem, smem, hbm, hbm, hbm, hbm, vm...  125 us

profile of v3, /device:TPU:1, one launch (start us, length us, event | category | flops | bytes accessed | tf_op | source)
XLA Modules:
  0.0 130.1 jit_solution(15587868638624697497)
XLA Ops:
  1.3 125.1 %judge.1 = (bf16[256,8192]{1,0:T(8,128)(2,1)S(1)}, f32[1,1]{1,0:T(1,128)}) custom-call(s32[1]{0:T(128)S(6)} %copy.12.plen_ref, s32[1,16]{1,0:T(1,128)} %routes_ref.1, bf16[16,128,2048]{2,1,0:T(8,128)(2,1)} %bitcast.7, bf16[512,128]{1,0:T(8,128)(2,1)} %bitcast.10, bf16[256,8192]{1,0:T(8,128)(2,1)} %bitcast.8, bf16[256,2048]{1,0:T(8,128)(2,1)} %bitcast.9, ...), custom_call_target="tpu_custom_call" | custom-call | tf_op jit(solution)/shard_map/judge/pallas_call | solution.py:311
  126.4 2.0 %copy.11 = bf16[1,1,256,8192]{3,2,1,0:T(8,128)(2,1)} copy(bf16[1,1,256,8192]{3,2,1,0:T(8,128)(2,1)S(1)} %bitcast.6) | data formatting | bytes 8388608

commit v4 on v3

--- a/solution.py
+++ b/solution.py
@@ -40,9 +40,8 @@
     n_slot = lax.axis_size("slot")
     n_prompt = lax.axis_size("prompt")
     x, y, c = me // 4, (me // 2) % 2, me % 2
-    chip = me // 2
     n_rows = keys.shape[0]
-    n_prefix = prefix.shape[2]
+    n_prefix = prefix.shape[3]
     n_suffix = suffix.shape[0]
     tile = image[0].shape[1]
     n_tiles = (n_rows - n_prefix - n_suffix) // tile
@@ -69,7 +68,7 @@
 
     load_queries = pltpu.make_async_copy(queries_ref, queries, local_sem.at[0])
     load_suffix = pltpu.make_async_copy(suffix_ref, suffix, local_sem.at[1])
-    load_prefix = pltpu.make_async_copy(prefix_ref, prefix.at[c, chip], local_sem.at[2])
+    load_prefix = pltpu.make_async_copy(prefix_ref, prefix.at[c, x, y], local_sem.at[2])
     for copy in stage(0) + stage(1):
         copy.start()
     load_prefix.start()
@@ -97,13 +96,34 @@
     routes[me] = flags
     pl.semaphore_wait(barrier, n_slot + n_prompt - 2)
 
-    for offset in OFFSETS:
-        if offset[2] == 0:
-            remote(
-                prefix_ref, prefix.at[c, chip], prefix_send, prefix_recv, slot=peer(offset)
-            ).start()
+    cut = n_prefix * 13 // 32
+    partner = peer((0, 1, 0))
+    along = [peer((k, 0, 0)) for k in (1, 3, 2)]
+    for target in along:
+        remote(
+            prefix_ref, prefix.at[c, x, y], prefix_send.at[0], prefix_recv.at[0], slot=target
+        ).start()
+    remote(
+        prefix_ref.at[pl.ds(0, cut)], prefix.at[c, x, y, pl.ds(0, cut)],
+        prefix_send.at[1], prefix_recv.at[1], slot=partner,
+    ).start()
     for offset in OFFSETS:
         remote(live, routes.at[me], route_send, route_recv, slot=peer(offset)).start()
+    whole = prefix.at[0, pl.ds(0, 3), 0]
+    below = prefix.at[0, 0, 0, pl.ds(0, cut)]
+    belows = prefix.at[0, pl.ds(0, 3), 0, pl.ds(0, cut)]
+    rests = prefix.at[c, :, y, pl.ds(cut, n_prefix - cut)]
+
+    def pass_prefix():
+        load_prefix.wait()
+        pltpu.make_async_copy(below, below, prefix_recv.at[1]).wait()
+        theirs = prefix.at[c, x, 1 - y, pl.ds(0, cut)]
+        for target in along:
+            remote(
+                theirs, theirs, prefix_send.at[2], prefix_recv.at[2], slot=target
+            ).start()
+        pltpu.make_async_copy(whole, whole, prefix_recv.at[0]).wait()
+        remote(rests, rests, prefix_send.at[3], prefix_recv.at[3], slot=partner).start()
 
     def send_tiles(g):
         for offset in OFFSETS:
@@ -124,13 +144,14 @@
         image[g][me] = staged[g][own_slot]
         if g > 0:
             send_tiles(g - 1)
+        if g == 1:
+            pass_prefix()
     send_tiles(KVH - 1)
     load_suffix.start()
     load_queries.start()
 
-    others = prefix.at[0, pl.ds(0, n_slot // 2 - 1)]
-    load_prefix.wait()
-    pltpu.make_async_copy(others, others, prefix_recv).wait()
+    pltpu.make_async_copy(belows, belows, prefix_recv.at[2]).wait()
+    pltpu.make_async_copy(rests, rests, prefix_recv.at[3]).wait()
     relay = remote(
         prefix.at[c], prefix.at[c], relay_sem.at[0], relay_sem.at[1], slot=me + 1 - 2 * c
     )
@@ -185,10 +206,12 @@
 
     def score_head(scores, h):
         at = pl.multiple_of(h * HD, HD)
-        scores[...] = lax.dot_general(
-            keys[...], queries[:, pl.ds(at, HD)], (((1,), (1,)), ((), ())),
-            preferred_element_type=jnp.float32,
-        )
+        query = queries[:, pl.ds(at, HD)]
+        for rows in (pl.ds(0, n_rows // 2), pl.ds(n_rows // 2, n_rows // 2)):
+            scores[rows, :] = lax.dot_general(
+                keys[rows, :], query, (((1,), (1,)), ((), ())),
+                preferred_element_type=jnp.float32,
+            )
 
     def mix_head(scores, h, score):
         seen = scores[:above, :]
@@ -211,8 +234,8 @@
             add_score(rounded[n_suffix - 8:, :], h)
 
     def build(g, pieces):
-        k_prefix = prefix[lax.rem(g, 2), g // 2].astype(jnp.float32)
-        v_prefix = prefix[lax.rem(g, 2), KVH // 2 + g // 2].astype(jnp.float32)
+        k_prefix = prefix[lax.rem(g, 2), g // 4, lax.rem(g // 2, 2)].astype(jnp.float32)
+        v_prefix = prefix[lax.rem(g, 2), 2 + g // 4, lax.rem(g // 2, 2)].astype(jnp.float32)
         inside = lax.broadcasted_iota(jnp.int32, (n_prefix, HD), 0) < plen_ref[0]
         keys[:n_prefix, :] = jnp.where(inside, k_prefix, k_prefix[0:1, :]).astype(jnp.bfloat16)
         values[:HD, :n_prefix] = jnp.where(inside, v_prefix, 0.0).T.astype(jnp.bfloat16)
@@ -292,7 +315,8 @@
     pltpu.make_async_copy(arrived_p, arrived_p, square_send).wait()
     sent = routes.at[pl.ds(0, n_slot - 1)]
     pltpu.make_async_copy(sent, sent, route_send).wait()
-    pltpu.make_async_copy(others, others, prefix_send).wait()
+    for k, done in enumerate((whole, below, belows, rests)):
+        pltpu.make_async_copy(done, done, prefix_send.at[k]).wait()
     for k in range(KVH):
         landed = image[k].at[pl.ds(0, n_slot - 1)]
         pltpu.make_async_copy(landed, landed, tile_send.at[k]).wait()
@@ -317,7 +341,7 @@
             jax.ShapeDtypeStruct((1, 1), jnp.float32),
         ],
         scratch_shapes=[pltpu.VMEM((n_slot, tile, 2 * HD), jnp.bfloat16)] * (3 * KVH) + [
-            pltpu.VMEM((2, n_slot // 2, n_prefix, HD), jnp.bfloat16),
+            pltpu.VMEM((2, n_slot // 4, 2, n_prefix, HD), jnp.bfloat16),
             pltpu.VMEM(suffix.shape, jnp.bfloat16),
             pltpu.VMEM(queries.shape, jnp.bfloat16),
             pltpu.VMEM((n_rows, HD), jnp.bfloat16),
@@ -333,7 +357,7 @@
             pltpu.VMEM((8, 128), jnp.float32),
             pltpu.VMEM((n_prompt, 8, 128), jnp.float32),
             dma((4,)), dma((KVH,)), dma((KVH,)), dma((KVH,)),
-            dma(()), dma(()), dma(()), dma(()), dma((2,)),
+            dma(()), dma(()), dma((4,)), dma((4,)), dma((2,)),
             dma(()), dma(()), dma(()), dma(()),
         ],
         compiler_params=pltpu.CompilerParams(

time: 130 us -> 129 us (level)
  Pallas kernels: 125 us -> 123 us
    pallas_call x1, Pallas kernels: 125 us -> 123 us  [judge(): pl.pallas_call(judge_kernel, in_specs=[smem, smem, hbm, hbm, hbm, hbm, vm...]
where the time goes in v4:
time: 129 us; the launch traced here: 128 us
  Pallas kernels  123 us (95%)
  between operations  2.97 us (2%)
  local copies, waits for them, and re-layouts  2.02 us (2%)
    pallas_call x1, Pallas kernels, judge(): pl.pallas_call(judge_kernel, in_specs=[smem, smem, hbm, hbm, hbm, hbm, vm...  123 us

profile of v4, /device:TPU:1, one launch (start us, length us, event | category | flops | bytes accessed | tf_op | source)
XLA Modules:
  0.0 128.3 jit_solution(15858230511044578908)
XLA Ops:
  1.3 123.3 %judge.1 = (bf16[256,8192]{1,0:T(8,128)(2,1)S(1)}, f32[1,1]{1,0:T(1,128)}) custom-call(s32[1]{0:T(128)S(6)} %copy.12.plen_ref, s32[1,16]{1,0:T(1,128)} %routes_ref.1, bf16[16,128,2048]{2,1,0:T(8,128)(2,1)} %bitcast.7, bf16[512,128]{1,0:T(8,128)(2,1)} %bitcast.10, bf16[256,8192]{1,0:T(8,128)(2,1)} %bitcast.8, bf16[256,2048]{1,0:T(8,128)(2,1)} %bitcast.9, ...), custom_call_target="tpu_custom_call" | custom-call | tf_op jit(solution)/shard_map/judge/pallas_call | solution.py:335
  124.6 2.0 %copy.11 = bf16[1,1,256,8192]{3,2,1,0:T(8,128)(2,1)} copy(bf16[1,1,256,8192]{3,2,1,0:T(8,128)(2,1)S(1)} %bitcast.6) | data formatting | bytes 8388608

commit v5 on v4

--- a/solution.py
+++ b/solution.py
@@ -94,6 +94,18 @@
             slots[d] = jnp.where(judge_of == d, jnp.int32(k), slots[d])
     live[...] = flags
     routes[me] = flags
+    def gather(g):
+        for copy in stage(g):
+            copy.wait()
+        if g + 2 < KVH:
+            for copy in stage(g + 2):
+                copy.start()
+        for d in range(n_slot):
+            packed[g][d] = staged[g][slots[d]]
+        image[g][me] = staged[g][own_slot]
+
+    gather(0)
+    gather(1)
     pl.semaphore_wait(barrier, n_slot + n_prompt - 2)
 
     cut = n_prefix * 13 // 32
@@ -133,19 +145,13 @@
                 slot=target,
             ).start()
 
-    for g in range(KVH):
-        for copy in stage(g):
-            copy.wait()
-        if g + 2 < KVH:
-            for copy in stage(g + 2):
-                copy.start()
-        for d in range(n_slot):
-            packed[g][d] = staged[g][slots[d]]
-        image[g][me] = staged[g][own_slot]
-        if g > 0:
+    send_tiles(0)
+    send_tiles(1)
+    pass_prefix()
+    for g in range(2, KVH):
+        gather(g)
+        if g > 2:
             send_tiles(g - 1)
-        if g == 1:
-            pass_prefix()
     send_tiles(KVH - 1)
     load_suffix.start()
     load_queries.start()

time: 129 us -> 126 us (0.977)
  Pallas kernels: 123 us -> 121 us
    pallas_call x1, Pallas kernels: 123 us -> 121 us  [judge(): pl.pallas_call(judge_kernel, in_specs=[smem, smem, hbm, hbm, hbm, hbm, vm...]
where the time goes in v5:
time: 126 us
  Pallas kernels  121 us (96%)
  between operations  2.97 us (2%)
  local copies, waits for them, and re-layouts  2.02 us (2%)
    pallas_call x1, Pallas kernels, judge(): pl.pallas_call(judge_kernel, in_specs=[smem, smem, hbm, hbm, hbm, hbm, vm...  121 us

profile of v5, /device:TPU:1, one launch (start us, length us, event | category | flops | bytes accessed | tf_op | source)
XLA Modules:
  0.0 125.8 jit_solution(13947897430698472289)
XLA Ops:
  1.3 120.8 %judge.1 = (bf16[256,8192]{1,0:T(8,128)(2,1)S(1)}, f32[1,1]{1,0:T(1,128)}) custom-call(s32[1]{0:T(128)S(6)} %copy.12.plen_ref, s32[1,16]{1,0:T(1,128)} %routes_ref.1, bf16[16,128,2048]{2,1,0:T(8,128)(2,1)} %bitcast.7, bf16[512,128]{1,0:T(8,128)(2,1)} %bitcast.10, bf16[256,8192]{1,0:T(8,128)(2,1)} %bitcast.8, bf16[256,2048]{1,0:T(8,128)(2,1)} %bitcast.9, ...), custom_call_target="tpu_custom_call" | custom-call | tf_op jit(solution)/shard_map/judge/pallas_call | solution.py:341
  122.1 2.0 %copy.11 = bf16[1,1,256,8192]{3,2,1,0:T(8,128)(2,1)} copy(bf16[1,1,256,8192]{3,2,1,0:T(8,128)(2,1)S(1)} %bitcast.6) | data formatting | bytes 8388608
